TPU v7x, 32 devices: a whole 2x2x4 slice. The times are simulated.
32 devices in a mesh: dp: 8 (over z, y), tensor: 4 (over x, core).
Axes of the slice: x: 2, y: 2, z: 4, core: 2. Of those that a mesh axis runs over, the one named last changes fastest.
Arguments:
- tokens: bfloat16 [4096, 2048], P(('dp', 'tensor')), may hold values from -6 to 6
- lengths: int32 [8, 4], P('dp'), may hold values from 0 to 512, as said below
- w_query: bfloat16 [2048, 2048], P(None, 'tensor'), may hold values from -0.125 to 0.125
- w_key: bfloat16 [2048, 2048], P(None, 'tensor'), may hold values from -0.125 to 0.125
- w_value: bfloat16 [2048, 2048], P(None, 'tensor'), may hold values from -0.125 to 0.125
- w_out: bfloat16 [2048, 2048], P('tensor'), may hold values from -0.125 to 0.125
- w_gate: bfloat16 [2048, 8192], P(None, 'tensor'), may hold values from -0.125 to 0.125
- w_up: bfloat16 [2048, 8192], P(None, 'tensor'), may hold values from -0.125 to 0.125
- w_down: bfloat16 [8192, 2048], P('tensor'), may hold values from -0.0625 to 0.0625
- gain_query: float32 [2048], P('tensor'), may hold values from 0.1 to 1.9
- gain_key: float32 [2048], P('tensor'), may hold values from 0.1 to 1.9
- gain_attn: float32 [2048], replicated, may hold values from 0.1 to 1.9
- gain_mlp: float32 [2048], replicated, may hold values from 0.1 to 1.9
- cotangent: bfloat16 [4096, 2048], P(('dp', 'tensor')), may hold values from -6 to 6
Outputs:
- output: bfloat16 [4096, 2048], P(('dp', 'tensor'))
- grad_tokens: bfloat16 [4096, 2048], P(('dp', 'tensor'))
- grad_w_query: float32 [2048, 2048], P('dp', 'tensor')
- grad_w_key: float32 [2048, 2048], P('dp', 'tensor')
- grad_w_value: float32 [2048, 2048], P('dp', 'tensor')
- grad_w_out: float32 [2048, 2048], P('tensor', 'dp')
- grad_w_gate: float32 [2048, 8192], P('dp', 'tensor')
- grad_w_up: float32 [2048, 8192], P('dp', 'tensor')
- grad_w_down: float32 [8192, 2048], P('tensor', 'dp')
- grad_gain_query: float32 [2048], P('tensor')
- grad_gain_key: float32 [2048], P('tensor')
- grad_gain_attn: float32 [2048], replicated
- grad_gain_mlp: float32 [2048], replicated
Inputs may be any that keep to these rules, and one draw needn't show every extreme that they name: Each row lists the lengths of its sequences in order, then zeros; every nonzero length is 128 or more and they sum to 512; row 0 holds one sequence of 512 tokens.
All inputs are finite; a program needn't handle non-finite values.
Results may differ from a plain program's by a relative error of at most 0.023.
Values may be sent and summed in bfloat16 or wider, within the bound.
A program may use at most 256 MiB of HBM per device.

v0:
```python
import math
import jax
import jax.numpy as jnp
from jax import lax
from jax.sharding import PartitionSpec as P

HD = 128
ROW_LEN = 512
EPS = 1e-06
THETA = 500000.0


def rotate(values, offsets, rot_sign):
    half_width = values.shape[-1] // 2
    frequency = jnp.exp(
        jnp.arange(half_width, dtype=jnp.float32) * (-2.0 * math.log(THETA) / values.shape[-1])
    )
    angles = offsets.astype(jnp.float32)[..., None, None] * frequency
    cosines = jnp.cos(angles)
    sine_part = rot_sign * jnp.sin(angles)
    first_half = values[..., :half_width]
    second_half = values[..., half_width:]
    return jnp.concatenate(
        [
            first_half * cosines - second_half * sine_part,
            second_half * cosines + first_half * sine_part,
        ],
        axis=-1,
    )


def row_layout(lengths_row):
    slots = jnp.arange(lengths_row.shape[0], dtype=jnp.int32)
    seq_ends = jnp.sum(jnp.where(slots[None, :] <= slots[:, None], lengths_row[None, :], 0), axis=1)
    position = jnp.arange(ROW_LEN, dtype=jnp.int32)
    passed = (position[:, None] >= seq_ends[None, :]).astype(jnp.int32)
    segment = jnp.sum(passed, axis=1)
    seq_start = jnp.sum(passed * lengths_row[None, :], axis=1)
    return (segment, position - seq_start)


def allowed_mask(segment):
    position = jnp.arange(segment.shape[0], dtype=jnp.int32)
    return (segment[:, None] == segment[None, :]) & (position[None, :] <= position[:, None])


def times_t(left_mat, right_mat):
    return lax.dot_general(
        left_mat, right_mat, (((1,), (1,)), ((), ())), preferred_element_type=jnp.float32
    )


def t_times(left_mat, right_mat):
    return lax.dot_general(
        left_mat, right_mat, (((0,), (0,)), ((), ())), preferred_element_type=jnp.float32
    )


def masked_scores(queries_low, keys_low, segment):
    scale_factor = 1.0 / math.sqrt(queries_low.shape[-1])
    scores = (
        jnp.einsum("qhd,khd->hqk", queries_low, keys_low, preferred_element_type=jnp.float32)
        * scale_factor
    )
    return jnp.where(allowed_mask(segment)[None], scores, -1e30)


def attend(block_item):
    queries_low, keys_low, values_low, segment = block_item
    scores = masked_scores(queries_low, keys_low, segment)
    row_max = jnp.max(scores, axis=-1, keepdims=True)
    shifted = jnp.exp(scores - row_max)
    row_total = jnp.sum(shifted, axis=-1, keepdims=True)
    attn_weights = (shifted / row_total).astype(jnp.bfloat16)
    mixed = jnp.einsum("hqk,khd->qhd", attn_weights, values_low, preferred_element_type=jnp.float32)
    return (mixed.astype(jnp.bfloat16), (row_max + jnp.log(row_total))[..., 0])


def attend_back(block_item):
    queries_low, keys_low, values_low, segment, log_total, grad_mixed = block_item
    scale_factor = 1.0 / math.sqrt(queries_low.shape[-1])
    scores = masked_scores(queries_low, keys_low, segment)
    attn_weights = jnp.exp(scores - log_total[..., None])
    grad_weights = jnp.einsum(
        "qhd,khd->hqk", grad_mixed, values_low, preferred_element_type=jnp.float32
    )
    row_dots = jnp.sum(attn_weights * grad_weights, axis=-1, keepdims=True)
    grad_scores = (attn_weights * (grad_weights - row_dots)).astype(jnp.bfloat16)
    grad_queries = scale_factor * jnp.einsum(
        "hqk,khd->qhd", grad_scores, keys_low, preferred_element_type=jnp.float32
    )
    grad_keys = scale_factor * jnp.einsum(
        "hqk,qhd->khd", grad_scores, queries_low, preferred_element_type=jnp.float32
    )
    grad_values = jnp.einsum(
        "hqk,qhd->khd",
        attn_weights.astype(jnp.bfloat16),
        grad_mixed,
        preferred_element_type=jnp.float32,
    )
    return (grad_queries, grad_keys, grad_values.astype(jnp.bfloat16))


def post_norm_back(grad_in, unit_rows, inv_scale, gain_vec):
    scaled = grad_in * gain_vec
    mean_dots = jnp.mean(scaled * unit_rows, axis=-1, keepdims=True)
    return (inv_scale * (scaled - unit_rows * mean_dots), jnp.sum(grad_in * unit_rows, axis=0))


OUTER = 4


def swap(value, shift):
    size = lax.axis_size("dp")
    return lax.ppermute(value, "dp", [(d, d ^ shift) for d in range(size)])


def pick(parts, index):
    return lax.dynamic_index_in_dim(parts, index, 0, keepdims=False)


def sum_inner(parts):
    inner = parts.shape[0]
    mine = lax.axis_index("dp") % inner
    total = pick(parts, mine)
    for k in range(1, inner):
        sent = pick(parts, mine ^ k).astype(jnp.bfloat16)
        total = total + swap(sent, k).astype(jnp.float32)
    return total


def trade_outer(parts, inner):
    mine = lax.axis_index("dp") // inner
    got = [(mine, pick(parts, mine))]
    for k in range(1, OUTER):
        got.append((mine ^ k, swap(pick(parts, mine ^ k), k * inner)))
    return got


def split_rows(grad, inner):
    cols = grad.shape[1]
    return grad.reshape(OUTER, inner, -1, cols).transpose(1, 0, 2, 3)


def split_cols(grad, inner):
    rows = grad.shape[0]
    return grad.reshape(rows, OUTER, inner, -1).transpose(2, 1, 0, 3)


def scatter_sum(parts, inner):
    half = sum_inner(parts).astype(jnp.bfloat16)
    got = trade_outer(half, inner)
    return sum((g.astype(jnp.float32) for _, g in got))


def scatter_join(parts, inner, axis):
    half = sum_inner(parts).astype(jnp.bfloat16)
    got = trade_outer(half, inner)
    stack = jnp.zeros((OUTER, *got[0][1].shape), jnp.bfloat16)
    for place, block in got:
        stack = lax.dynamic_update_index_in_dim(stack, block, place, 0)
    joined = jnp.concatenate([stack[z] for z in range(OUTER)], axis=axis)
    return joined.astype(jnp.float32)


def body(
    tokens,
    lengths,
    w_query,
    w_key,
    w_value,
    w_out,
    w_gate,
    w_up,
    w_down,
    gain_query,
    gain_key,
    gain_attn,
    gain_mlp,
    cotangent,
):
    rows_dev = lengths.shape[0]
    model_width = w_query.shape[0]
    local_width = w_query.shape[1]
    head_count = local_width // HD
    gathered = lax.all_gather(tokens, "tensor", axis=0, tiled=True)
    row_count = gathered.shape[0]
    segment, offsets = jax.vmap(row_layout)(lengths)
    queries = jnp.dot(gathered, w_query, preferred_element_type=jnp.float32)
    keys_raw = jnp.dot(gathered, w_key, preferred_element_type=jnp.float32)
    values_low = jnp.dot(gathered, w_value, preferred_element_type=jnp.float32).astype(jnp.bfloat16)
    q_total, k_total = lax.psum(
        (jnp.sum(queries * queries, axis=1), jnp.sum(keys_raw * keys_raw, axis=1)), "tensor"
    )
    q_inv = lax.rsqrt(q_total / model_width + EPS)[:, None]
    k_inv = lax.rsqrt(k_total / model_width + EPS)[:, None]
    q_unit = queries * q_inv
    k_unit = keys_raw * k_inv

    def to_heads(values):
        return values.reshape(rows_dev, ROW_LEN, head_count, HD)

    queries_low = rotate(to_heads(q_unit * gain_query), offsets, 1.0).astype(jnp.bfloat16)
    keys_low = rotate(to_heads(k_unit * gain_key), offsets, 1.0).astype(jnp.bfloat16)
    values_heads = to_heads(values_low)
    mixed_heads, log_total = jax.vmap(lambda *a: attend(a))(
        queries_low, keys_low, values_heads, segment
    )
    mixed_low = mixed_heads.reshape(row_count, local_width)
    attn_out = lax.psum_scatter(
        jnp.dot(mixed_low, w_out, preferred_element_type=jnp.float32).astype(jnp.bfloat16),
        "tensor",
        scatter_dimension=0,
        tiled=True,
    ).astype(jnp.float32)
    a_inv = lax.rsqrt(jnp.mean(attn_out * attn_out, axis=1, keepdims=True) + EPS)
    a_unit = attn_out * a_inv
    hidden = tokens.astype(jnp.float32) + a_unit * gain_attn
    hidden_low = hidden.astype(jnp.bfloat16)
    hidden_all = lax.all_gather(hidden_low, "tensor", axis=0, tiled=True)
    inner_count = lax.axis_size("dp") // OUTER
    outer_index = lax.axis_index("dp") // inner_count

    def gather_group(shard):
        groups = [[z * inner_count + i for z in range(OUTER)] for i in range(inner_count)]
        part = lax.all_gather(shard, "dp", axis=0, tiled=True, axis_index_groups=groups)
        return lax.all_gather(part, "tensor", axis=0, tiled=True)

    hidden_group = gather_group(hidden_low)
    gate_acts = jnp.dot(hidden_all, w_gate, preferred_element_type=jnp.float32)
    up_acts = jnp.dot(hidden_all, w_up, preferred_element_type=jnp.float32)
    gate_sigmoid = jax.nn.sigmoid(gate_acts)
    inner_low = (gate_acts * gate_sigmoid * up_acts).astype(jnp.bfloat16)
    mlp_out = lax.psum_scatter(
        jnp.dot(inner_low, w_down, preferred_element_type=jnp.float32).astype(jnp.bfloat16),
        "tensor",
        scatter_dimension=0,
        tiled=True,
    ).astype(jnp.float32)
    f_inv = lax.rsqrt(jnp.mean(mlp_out * mlp_out, axis=1, keepdims=True) + EPS)
    f_unit = mlp_out * f_inv
    output = (hidden + f_unit * gain_mlp).astype(jnp.bfloat16)
    grad_output = cotangent.astype(jnp.float32)
    grad_mlp, grad_gain_mlp_part = post_norm_back(grad_output, f_unit, f_inv, gain_mlp)
    grad_mlp_low = grad_mlp.astype(jnp.bfloat16)
    mlp_grad_all = lax.all_gather(grad_mlp_low, "tensor", axis=0, tiled=True)
    mlp_grad_group = gather_group(grad_mlp_low)
    grad_inner = times_t(mlp_grad_all, w_down)
    grad_gate_low = (
        grad_inner * up_acts * gate_sigmoid * (1.0 + gate_acts * (1.0 - gate_sigmoid))
    ).astype(jnp.bfloat16)
    grad_up_low = (grad_inner * gate_acts * gate_sigmoid).astype(jnp.bfloat16)
    part_width = w_gate.shape[1] // OUTER
    gate_part = lax.dynamic_slice_in_dim(w_gate, outer_index * part_width, part_width, 1)
    up_part = lax.dynamic_slice_in_dim(w_up, outer_index * part_width, part_width, 1)
    down_part = lax.dynamic_slice_in_dim(w_down, outer_index * part_width, part_width, 0)
    gate_g = jnp.dot(hidden_group, gate_part, preferred_element_type=jnp.float32)
    up_g = jnp.dot(hidden_group, up_part, preferred_element_type=jnp.float32)
    sig_g = jax.nn.sigmoid(gate_g)
    inner_g = (gate_g * sig_g * up_g).astype(jnp.bfloat16)
    grad_inner_g = times_t(mlp_grad_group, down_part)
    grad_gate_g = (grad_inner_g * up_g * sig_g * (1.0 + gate_g * (1.0 - sig_g))).astype(
        jnp.bfloat16
    )
    grad_up_g = (grad_inner_g * gate_g * sig_g).astype(jnp.bfloat16)
    sum_down = scatter_join(
        split_cols(t_times(inner_g, mlp_grad_group), inner_count), inner_count, 0
    )
    sum_gate = scatter_join(
        split_rows(t_times(hidden_group, grad_gate_g), inner_count), inner_count, 1
    )
    sum_up = scatter_join(split_rows(t_times(hidden_group, grad_up_g), inner_count), inner_count, 1)
    grad_hidden = grad_output + lax.psum_scatter(
        (times_t(grad_gate_low, w_gate) + times_t(grad_up_low, w_up)).astype(jnp.bfloat16),
        "tensor",
        scatter_dimension=0,
        tiled=True,
    ).astype(jnp.float32)
    grad_attn, grad_gain_attn_part = post_norm_back(grad_hidden, a_unit, a_inv, gain_attn)
    attn_grad_all = lax.all_gather(grad_attn.astype(jnp.bfloat16), "tensor", axis=0, tiled=True)
    grad_w_out = t_times(mixed_low, attn_grad_all)
    grad_mixed = times_t(attn_grad_all, w_out).astype(jnp.bfloat16)
    grad_q_rot, grad_k_rot, grad_values_low = jax.vmap(lambda *a: attend_back(a))(
        queries_low, keys_low, values_heads, segment, log_total, to_heads(grad_mixed)
    )
    grad_q_norm = rotate(grad_q_rot, offsets, -1.0).reshape(row_count, local_width)
    grad_k_norm = rotate(grad_k_rot, offsets, -1.0).reshape(row_count, local_width)
    grad_gain_query_part = jnp.sum(grad_q_norm * q_unit, axis=0)
    grad_gain_key_part = jnp.sum(grad_k_norm * k_unit, axis=0)
    q_scaled = grad_q_norm * gain_query
    k_scaled = grad_k_norm * gain_key
    q_dots, k_dots = lax.psum(
        (jnp.sum(q_scaled * q_unit, axis=1), jnp.sum(k_scaled * k_unit, axis=1)), "tensor"
    )
    grad_queries_low = (q_inv * (q_scaled - q_unit * (q_dots / model_width)[:, None])).astype(
        jnp.bfloat16
    )
    grad_keys_low = (k_inv * (k_scaled - k_unit * (k_dots / model_width)[:, None])).astype(
        jnp.bfloat16
    )
    grad_values_flat = grad_values_low.reshape(row_count, local_width)
    grad_w_query = t_times(gathered, grad_queries_low)
    grad_w_key = t_times(gathered, grad_keys_low)
    grad_w_value = t_times(gathered, grad_values_flat)
    grad_tokens = (
        grad_hidden
        + lax.psum_scatter(
            (
                times_t(grad_queries_low, w_query)
                + times_t(grad_keys_low, w_key)
                + times_t(grad_values_flat, w_value)
            ).astype(jnp.bfloat16),
            "tensor",
            scatter_dimension=0,
            tiled=True,
        ).astype(jnp.float32)
    ).astype(jnp.bfloat16)
    tensor_start = lax.axis_index("tensor") * local_width
    zero_row = jnp.zeros((model_width,), jnp.float32)
    q_full = lax.dynamic_update_slice(zero_row, grad_gain_query_part, (tensor_start,))
    k_full = lax.dynamic_update_slice(zero_row, grad_gain_key_part, (tensor_start,))
    gain_stack = jnp.stack([q_full, k_full, grad_gain_attn_part, grad_gain_mlp_part])
    gain_total = lax.psum(gain_stack, ("dp", "tensor"))
    grad_gain_query = lax.dynamic_slice(gain_total[0], (tensor_start,), (local_width,))
    grad_gain_key = lax.dynamic_slice(gain_total[1], (tensor_start,), (local_width,))
    summed = (
        scatter_sum(split_rows(grad_w_query, inner_count), inner_count),
        scatter_sum(split_rows(grad_w_key, inner_count), inner_count),
        scatter_sum(split_rows(grad_w_value, inner_count), inner_count),
        scatter_sum(split_cols(grad_w_out, inner_count), inner_count),
        sum_gate,
        sum_up,
        sum_down,
    )
    return (
        output,
        grad_tokens,
        summed[0],
        summed[1],
        summed[2],
        summed[3],
        summed[4],
        summed[5],
        summed[6],
        grad_gain_query,
        grad_gain_key,
        gain_total[2],
        gain_total[3],
    )


def solution(mesh):
    placed = (
        P(("dp", "tensor"), None),
        P("dp", None),
        P(None, "tensor"),
        P(None, "tensor"),
        P(None, "tensor"),
        P("tensor", None),
        P(None, "tensor"),
        P(None, "tensor"),
        P("tensor", None),
        P("tensor"),
        P("tensor"),
        P(),
        P(),
        P(("dp", "tensor"), None),
    )
    return jax.shard_map(
        body,
        mesh=mesh,
        in_specs=placed,
        out_specs=(
            P(("dp", "tensor"), None),
            P(("dp", "tensor"), None),
            P("dp", "tensor"),
            P("dp", "tensor"),
            P("dp", "tensor"),
            P("tensor", "dp"),
            P("dp", "tensor"),
            P("dp", "tensor"),
            P("tensor", "dp"),
            P("tensor"),
            P("tensor"),
            P(),
            P(),
        ),
        check_vma=False,
    )
```

profile of v0, /device:TPU:9, one launch (start us, length us, event | category | flops | bytes accessed | tf_op | source)
XLA Modules:
  0.0 888.0 jit_solution(406805340475882868)
XLA Ops:
  12.2 21.6 %all-gather.9.cloned.1.call-done = bf16[512,2048]{1,0:T(8,128)(2,1)} async-done(((bf16[128,2048]{1,0:T(8,128)(2,1)}), bf16[512,2048]{1,0:T(8,128)(2,1)}) %all-gather.9.cloned.1.call-update) | async-done | bytes 2097168 | tf_op jit(solution)/shard_map/all_gather | solution.py:186
  39.1 5.3 all-reduce.1
  70.3 32.8 %reduce-scatter.5.cloned.1.call-done = bf16[128,2048]{1,0:T(8,128)(2,1)} async-done(((bf16[512,2048]{1,0:T(8,128)(2,1)}), bf16[128,2048]{1,0:T(8,128)(2,1)}) %reduce-scatter.5.cloned.1.call-update) | async-done | bytes 524304 | tf_op jit(solution)/shard_map/reduce_scatter | solution.py:210
  106.8 22.8 %all-gather.11.cloned.1.call-done = bf16[512,2048]{1,0:T(8,128)(2,1)} async-done(((bf16[128,2048]{1,0:T(8,128)(2,1)}), bf16[512,2048]{1,0:T(8,128)(2,1)}) %all-gather.11.cloned.1.call-update) | async-done | bytes 2097168 | tf_op jit(solution)/shard_map/all_gather | solution.py:220
  129.6 8.6 fusion.92
  138.2 8.4 fusion.93
  148.6 9.5 %convolution_convert_fusion = bf16[512,2048]{1,0:T(8,128)(2,1)} fusion(bf16[2048,2048]{1,0:T(8,128)(2,1)} %param.22, f32[512,2048]{1,0:T(8,128)S(1)} %fusion.93, f32[512,2048]{1,0:T(8,128)S(1)} %fusion.92), kind=kOutput, calls=%fused_computation.21 | convolution fusion | flops 4302307328 | bytes 18874368 | tf_op jit(solution)/shard_map/dot_general | solution.py:235
  158.2 31.1 %reduce-scatter.7.cloned.1.call-done = bf16[128,2048]{1,0:T(8,128)(2,1)} async-done(((bf16[512,2048]{1,0:T(8,128)(2,1)}), bf16[128,2048]{1,0:T(8,128)(2,1)}) %reduce-scatter.7.cloned.1.call-update) | async-done | bytes 524304 | tf_op jit(solution)/shard_map/reduce_scatter | solution.py:234
  194.3 23.1 %all-gather.13.cloned.1.call-done = bf16[512,2048]{1,0:T(8,128)(2,1)} async-done(((bf16[128,2048]{1,0:T(8,128)(2,1)}), bf16[512,2048]{1,0:T(8,128)(2,1)}) %all-gather.13.cloned.1.call-update) | async-done | bytes 2097168 | tf_op jit(solution)/shard_map/all_gather | solution.py:246
  217.4 7.6 fusion.94
  225.0 13.6 %fusion.25 = f32[512,2048]{1,0:T(8,128)} fusion(bf16[2048,2048]{1,0:T(8,128)(2,1)} %param.20, f32[512,2048]{1,0:T(8,128)} %copy-done.53, f32[512,2048]{1,0:T(8,128)S(1)} %fusion.94, f32[512,2048]{1,0:T(8,128)} %copy-done.54), kind=kOutput, calls=%fused_computation.56 | convolution fusion | flops 4305453056 | bytes 25165824 | tf_op jit(solution)/shard_map/dot_general | solution.py:48
  238.6 11.8 %add_convert_fusion.1 = bf16[512,2048]{1,0:T(8,128)(2,1)} fusion(f32[512,2048]{1,0:T(8,128)} %fusion.25, bf16[2048,2048]{1,0:T(8,128)(2,1)} %param.21, f32[512,2048]{1,0:T(8,128)S(1)} %fusion.94, f32[512,2048]{1,0:T(8,128)} %copy-done.53), kind=kOutput, calls=%fused_computation.8 | convolution fusion | flops 4303355904 | bytes 23068672 | tf_op jit(solution)/shard_map/dot_general | solution.py:48
  251.3 30.4 %reduce-scatter.9.cloned.1.call-done = bf16[128,2048]{1,0:T(8,128)(2,1)} async-done(((bf16[512,2048]{1,0:T(8,128)(2,1)}), bf16[128,2048]{1,0:T(8,128)(2,1)}) %reduce-scatter.9.cloned.1.call-update) | async-done | bytes 524304 | tf_op jit(solution)/shard_map/reduce_scatter | solution.py:273
  286.9 41.1 %all-gather.17.cloned.1.call-done = bf16[512,2048]{1,0:T(8,128)(2,1)} async-done(((bf16[128,2048]{1,0:T(8,128)(2,1)}), bf16[512,2048]{1,0:T(8,128)(2,1)}) %all-gather.17.cloned.1.call-update) | async-done | bytes 2097168 | tf_op jit(solution)/shard_map/all_gather | solution.py:226
  328.2 25.5 %all-gather.15.cloned.1.call-done = bf16[512,2048]{1,0:T(8,128)(2,1)} async-done(((bf16[128,2048]{1,0:T(8,128)(2,1)}), bf16[512,2048]{1,0:T(8,128)(2,1)}) %all-gather.15.cloned.1.call-update) | async-done | bytes 2097168 | tf_op jit(solution)/shard_map/all_gather | solution.py:280
  378.0 5.7 all-reduce
  399.8 60.7 %all-gather.19.cloned.1.call-done = bf16[2048,2048]{1,0:T(8,128)(2,1)} async-done(((bf16[512,2048]{1,0:T(8,128)(2,1)}), bf16[2048,2048]{1,0:T(8,128)(2,1)}) %all-gather.19.cloned.1.call-update) | async-done | bytes 8388624 | tf_op jit(solution)/shard_map/all_gather | solution.py:227
  460.5 10.6 %fusion.14 = f32[2048,512]{1,0:T(8,128)} fusion(bf16[2048,2048]{1,0:T(8,128)(2,1)} %all-gather.19.cloned.1.call-done, bf16[2048,2048]{1,0:T(8,128)(2,1)} %param.20, s32[]{:T(128)S(6)} %select_n.141), kind=kOutput, calls=%fused_computation.44 | convolution fusion | flops 4294967296 | bytes 14680068 | tf_op jit(solution)/shard_map/dot_general | solution.py:257
  471.2 8.7 fusion.18
  483.0 6.6 reshape.572
  489.7 5.4 constant_dynamic-slice_fusion.8
  495.1 5.8 copy.99
  505.5 6.8 reshape.573
  512.2 5.5 constant_dynamic-slice_fusion.6
  517.7 5.8 copy.100
  527.1 6.8 reshape.574
  554.8 71.2 %psum.39 = f32[4,2048]{1,0:T(4,128)S(1)} all-reduce(f32[4,2048]{1,0:T(4,128)S(1)} %pad_maximum_fusion.8), channel_id=1, replica_groups=mesh['dp'=8,'tensor'=4] {'dp','tensor'}, use_global_device_ids=true, to_apply=%region_26.27 | all-reduce | flops 8192 | bytes 65536 | tf_op jit(solution)/shard_map/psum | solution.py:323
  626.7 5.4 constant_dynamic-slice_fusion.5
  632.7 4.4 copy.71
  637.1 6.0 copy.73
  643.1 4.6 copy.75
  662.5 5.7 collective-permute-done.3
  668.2 14.5 %collective-permute-done.2 = bf16[256,512]{1,0:T(8,128)(2,1)S(1)} collective-permute-done((bf16[256,512]{1,0:T(8,128)(2,1)S(1)}, bf16[256,512]{1,0:T(8,128)(2,1)S(1)}, u32[]{:S(2)}, u32[]{:S(2)}) %collective-permute-start.2) | collective-permute-done | bytes 262176 | tf_op jit(solution)/shard_map/ppermute | solution.py:115
  683.8 4.6 collective-permute-start.10
  688.4 13.6 %collective-permute-done.7 = bf16[256,512]{1,0:T(8,128)(2,1)S(1)} collective-permute-done((bf16[256,512]{1,0:T(8,128)(2,1)S(1)}, bf16[256,512]{1,0:T(8,128)(2,1)S(1)}, u32[]{:S(2)}, u32[]{:S(2)}) %collective-permute-start.7) | collective-permute-done | bytes 262176 | tf_op jit(solution)/shard_map/ppermute | solution.py:115
  710.9 13.6 %collective-permute-done.11 = bf16[256,512]{1,0:T(8,128)(2,1)S(1)} collective-permute-done((bf16[256,512]{1,0:T(8,128)(2,1)S(1)}, bf16[256,512]{1,0:T(8,128)(2,1)S(1)}, u32[]{:S(2)}, u32[]{:S(2)}) %collective-permute-start.11) | collective-permute-done | bytes 262176 | tf_op jit(solution)/shard_map/ppermute | solution.py:115
  729.3 6.5 collective-permute-done.15
  742.6 7.8 fusion.20
  750.4 7.7 fusion.26
  760.4 8.2 fusion.4
  772.6 9.7 %fusion.5 = f32[512,2048]{1,0:T(8,128)} fusion(bf16[2048,2048]{1,0:T(8,128)(2,1)S(1)} %bitcast.317, f32[2048,512]{1,0:T(8,128)} %fusion.18, f32[2048,512]{1,0:T(8,128)} %fusion.14), kind=kOutput, calls=%fused_computation.25 | convolution fusion | flops 4301258752 | bytes 20971520 | tf_op jit(solution)/shard_map/dot_general | solution.py:54
  782.3 6.9 reshape.577
  789.2 4.2 constant_dynamic-slice_fusion.1
  807.9 18.9 %collective-permute-done.24 = bf16[4,512,256]{2,1,0:T(8,128)(2,1)S(1)} collective-permute-done((bf16[4,512,256]{2,1,0:T(8,128)(2,1)S(1)}, bf16[4,512,256]{2,1,0:T(8,128)(2,1)S(1)}, u32[]{:S(2)}, u32[]{:S(2)}) %collective-permute-start.24) | collective-permute-done | bytes 1048608 | tf_op jit(solution)/shard_map/ppermute | solution.py:115
  834.6 14.9 %collective-permute-done.22 = bf16[256,512]{1,0:T(8,128)(2,1)S(1)} collective-permute-done((bf16[256,512]{1,0:T(8,128)(2,1)S(1)}, bf16[256,512]{1,0:T(8,128)(2,1)S(1)}, u32[]{:S(2)}, u32[]{:S(2)}) %collective-permute-start.22) | collective-permute-done | bytes 262176 | tf_op jit(solution)/shard_map/ppermute | solution.py:115
  849.5 15.1 %collective-permute-done.23 = bf16[256,512]{1,0:T(8,128)(2,1)S(1)} collective-permute-done((bf16[256,512]{1,0:T(8,128)(2,1)S(1)}, bf16[256,512]{1,0:T(8,128)(2,1)S(1)}, u32[]{:S(2)}, u32[]{:S(2)}) %collective-permute-start.23) | collective-permute-done | bytes 262176 | tf_op jit(solution)/shard_map/ppermute | solution.py:115
  864.8 4.3 collective-permute-done.26
  869.3 6.6 collective-permute-done.27
  (310 shorter events, 196.2 us)
Async XLA Ops:
  7.2 26.6 %copy-start = (bf16[2048,512]{1,0:T(8,128)(2,1)S(1)}, bf16[2048,512]{1,0:T(8,128)(2,1)}, u32[]{:S(2)}) copy-start(bf16[2048,512]{1,0:T(8,128)(2,1)} %param.16) | copy-start | bytes 6291460
  7.2 26.6 %all-gather.9.cloned.1.call-start = ((), (), s32[]{:S(2)}) async-start(), calls=%async_computation.4 | async-start | bytes 2621440 | tf_op jit(solution)/shard_map/all_gather | solution.py:186
  7.9 95.1 %reduce-scatter.5.cloned.1.call-start = ((), (), s32[]{:S(2)}) async-start(), calls=%async_computation.5 | async-start | bytes 2621440 | tf_op jit(solution)/shard_map/reduce_scatter | solution.py:210
  66.8 37.5 %copy-start.44 = (bf16[4,128,512]{2,1,0:T(8,128)(2,1)}, bf16[4,128,512]{2,1,0:T(8,128)(2,1)S(1)}, u32[]{:S(2)}) copy-start(bf16[4,128,512]{2,1,0:T(8,128)(2,1)S(1)} %fusion.40) | copy-start | bytes 1572868
  67.6 36.7 %copy-start.19 = (bf16[128,2048]{1,0:T(8,128)(2,1)S(1)}, bf16[128,2048]{1,0:T(8,128)(2,1)}, u32[]{:S(2)}) copy-start(bf16[128,2048]{1,0:T(8,128)(2,1)} %param.14) | copy-start | bytes 1572868
  67.6 36.7 %copy-start.46 = (f32[2048]{0:T(1024)S(1)}, f32[2048]{0:T(1024)}, u32[]{:S(2)}) copy-start(f32[2048]{0:T(1024)} %param.25) | copy-start | bytes 24580
  70.2 59.4 %all-gather.11.cloned.1.call-start = ((), (), s32[]{:S(2)}) async-start(), calls=%async_computation.6 | async-start | bytes 2621440 | tf_op jit(solution)/shard_map/all_gather | solution.py:220
  106.4 82.9 %reduce-scatter.7.cloned.1.call-start = ((), (), s32[]{:S(2)}) async-start(), calls=%async_computation.7 | async-start | bytes 2621440 | tf_op jit(solution)/shard_map/reduce_scatter | solution.py:234
  148.6 41.9 %copy-start.11 = (bf16[128,2048]{1,0:T(8,128)(2,1)S(1)}, bf16[128,2048]{1,0:T(8,128)(2,1)}, u32[]{:S(2)}) copy-start(bf16[128,2048]{1,0:T(8,128)(2,1)} %param.27) | copy-start | bytes 1572868
  148.6 41.9 %copy-start.47 = (f32[2048]{0:T(1024)S(1)}, f32[2048]{0:T(1024)}, u32[]{:S(2)}) copy-start(f32[2048]{0:T(1024)} %param.26) | copy-start | bytes 24580
  158.1 59.3 %all-gather.13.cloned.1.call-start = ((), (), s32[]{:S(2)}) async-start(), calls=%async_computation.8 | async-start | bytes 2621440 | tf_op jit(solution)/shard_map/all_gather | solution.py:246
  194.2 87.4 %reduce-scatter.9.cloned.1.call-start = ((), (), s32[]{:S(2)}) async-start(), calls=%async_computation.9 | async-start | bytes 2621440 | tf_op jit(solution)/shard_map/reduce_scatter | solution.py:273
  238.6 43.0 %copy-start.16 = (bf16[128,2048]{1,0:T(8,128)(2,1)S(1)}, bf16[128,2048]{1,0:T(8,128)(2,1)}, u32[]{:S(2)}) copy-start(bf16[128,2048]{1,0:T(8,128)(2,1)} %reduce-scatter.5.cloned.1.call-done) | copy-start | bytes 1572868
  250.5 77.5 %all-gather.17.cloned.1.call-start = ((), (), s32[]{:S(2)}) async-start(), calls=%async_computation.12 | async-start | bytes 2621440 | tf_op jit(solution)/shard_map/all_gather | solution.py:226
  251.2 102.6 %all-gather.15.cloned.1.call-start = ((), (), s32[]{:S(2)}) async-start(), calls=%async_computation.10 | async-start | bytes 2621440 | tf_op jit(solution)/shard_map/all_gather | solution.py:280
  286.1 113.6 %all-gather.21.cloned.1.call-start = ((), (), s32[]{:S(2)}) async-start(), calls=%async_computation.14 | async-start | bytes 2621440 | tf_op jit(solution)/shard_map/all_gather | solution.py:226
  286.9 173.7 %all-gather.19.cloned.1.call-start = ((), (), s32[]{:S(2)}) async-start(), calls=%async_computation.13 | async-start | bytes 10485760 | tf_op jit(solution)/shard_map/all_gather | solution.py:227
  328.0 412.5 %reduce-scatter.11.cloned.1.call-start = ((), (), s32[]{:S(2)}) async-start(), calls=%async_computation.11 | async-start | bytes 2621440 | tf_op jit(solution)/shard_map/reduce_scatter | solution.py:307
  395.6 347.0 %all-gather.23.cloned.1.call-start = ((), (), s32[]{:S(2)}) async-start(), calls=%async_computation.15 | async-start | bytes 10485760 | tf_op jit(solution)/shard_map/all_gather | solution.py:227
  500.9 147.4 %collective-permute-start = (bf16[4,256,512]{2,1,0:T(8,128)(2,1)}, bf16[4,256,512]{2,1,0:T(8,128)(2,1)}, u32[]{:S(2)}, u32[]{:S(2)}) collective-permute-start(bf16[4,256,512]{2,1,0:T(8,128)(2,1)} %bitcast.298), channel_id=1, source_target_pairs={{0,4},{4,0},{8,12},{12,8},{16,20},{20,16},{24,28},{28,24},{1,5},{5... | collective-permute-start | bytes 3145736 | tf_op jit(solution)/shard_map/ppermute | solution.py:115
  523.5 130.4 %collective-permute-start.4 = (bf16[4,256,512]{2,1,0:T(8,128)(2,1)}, bf16[4,256,512]{2,1,0:T(8,128)(2,1)}, u32[]{:S(2)}, u32[]{:S(2)}) collective-permute-start(bf16[4,256,512]{2,1,0:T(8,128)(2,1)} %bitcast.297), channel_id=1, source_target_pairs={{0,4},{4,0},{8,12},{12,8},{16,20},{20,16},{24,28},{28,24},{1,5},{5... | collective-permute-start | bytes 3145736 | tf_op jit(solution)/shard_map/ppermute | solution.py:115
  542.2 113.6 %collective-permute-start.8 = (bf16[4,256,512]{2,1,0:T(8,128)(2,1)}, bf16[4,256,512]{2,1,0:T(8,128)(2,1)}, u32[]{:S(2)}, u32[]{:S(2)}) collective-permute-start(bf16[4,256,512]{2,1,0:T(8,128)(2,1)} %bitcast.296), channel_id=1, source_target_pairs={{0,4},{4,0},{8,12},{12,8},{16,20},{20,16},{24,28},{28,24},{1,5},{5... | collective-permute-start | bytes 3145736 | tf_op jit(solution)/shard_map/ppermute | solution.py:115
  548.5 109.2 %collective-permute-start.12 = (bf16[4,512,256]{2,1,0:T(8,128)(2,1)}, bf16[4,512,256]{2,1,0:T(8,128)(2,1)}, u32[]{:S(2)}, u32[]{:S(2)}) collective-permute-start(bf16[4,512,256]{2,1,0:T(8,128)(2,1)} %fusion.56), channel_id=1, source_target_pairs={{0,4},{4,0},{8,12},{12,8},{16,20},{20,16},{24,28},{28,24},{1,5},{5... | collective-permute-start | bytes 3145736 | tf_op jit(solution)/shard_map/ppermute | solution.py:115
  650.6 17.6 %collective-permute-start.3 = (bf16[256,512]{1,0:T(8,128)(2,1)S(1)}, bf16[256,512]{1,0:T(8,128)(2,1)S(1)}, u32[]{:S(2)}, u32[]{:S(2)}) collective-permute-start(bf16[256,512]{1,0:T(8,128)(2,1)S(1)} %get-tuple-element.69), channel_id=1, source_target_pairs={{0,24},{4,28},{8,16},{12,20},{16,8},{20,12},{24,0},{28,4},{1,25},{... | collective-permute-start | bytes 786440 | tf_op jit(solution)/shard_map/ppermute | solution.py:115
  651.0 31.7 %collective-permute-start.2 = (bf16[256,512]{1,0:T(8,128)(2,1)S(1)}, bf16[256,512]{1,0:T(8,128)(2,1)S(1)}, u32[]{:S(2)}, u32[]{:S(2)}) collective-permute-start(bf16[256,512]{1,0:T(8,128)(2,1)S(1)} %get-tuple-element.70), channel_id=1, source_target_pairs={{0,16},{4,20},{8,24},{12,28},{16,0},{20,4},{24,8},{28,12},{1,17},{... | collective-permute-start | bytes 786440 | tf_op jit(solution)/shard_map/ppermute | solution.py:115
  653.9 30.0 %collective-permute-start.1 = (bf16[256,512]{1,0:T(8,128)(2,1)S(1)}, bf16[256,512]{1,0:T(8,128)(2,1)S(1)}, u32[]{:S(2)}, u32[]{:S(2)}) collective-permute-start(bf16[256,512]{1,0:T(8,128)(2,1)S(1)} %get-tuple-element.68), channel_id=1, source_target_pairs={{0,8},{4,12},{8,0},{12,4},{16,24},{20,28},{24,16},{28,20},{1,9},{5... | collective-permute-start | bytes 786440 | tf_op jit(solution)/shard_map/ppermute | solution.py:115
  655.7 46.2 %collective-permute-start.7 = (bf16[256,512]{1,0:T(8,128)(2,1)S(1)}, bf16[256,512]{1,0:T(8,128)(2,1)S(1)}, u32[]{:S(2)}, u32[]{:S(2)}) collective-permute-start(bf16[256,512]{1,0:T(8,128)(2,1)S(1)} %get-tuple-element.66), channel_id=1, source_target_pairs={{0,24},{4,28},{8,16},{12,20},{16,8},{20,12},{24,0},{28,4},{1,25},{... | collective-permute-start | bytes 786440 | tf_op jit(solution)/shard_map/ppermute | solution.py:115
  657.8 48.1 %collective-permute-start.6 = (bf16[256,512]{1,0:T(8,128)(2,1)S(1)}, bf16[256,512]{1,0:T(8,128)(2,1)S(1)}, u32[]{:S(2)}, u32[]{:S(2)}) collective-permute-start(bf16[256,512]{1,0:T(8,128)(2,1)S(1)} %get-tuple-element.67), channel_id=1, source_target_pairs={{0,16},{4,20},{8,24},{12,28},{16,0},{20,4},{24,8},{28,12},{1,17},{... | collective-permute-start | bytes 786440 | tf_op jit(solution)/shard_map/ppermute | solution.py:115
  662.5 78.0 %copy-start.22 = (bf16[128,2048]{1,0:T(8,128)(2,1)S(1)}, bf16[128,2048]{1,0:T(8,128)(2,1)}, u32[]{:S(2)}) copy-start(bf16[128,2048]{1,0:T(8,128)(2,1)} %reduce-scatter.9.cloned.1.call-done) | copy-start | bytes 1572868
  668.2 38.7 %collective-permute-start.5 = (bf16[256,512]{1,0:T(8,128)(2,1)S(1)}, bf16[256,512]{1,0:T(8,128)(2,1)S(1)}, u32[]{:S(2)}, u32[]{:S(2)}) collective-permute-start(bf16[256,512]{1,0:T(8,128)(2,1)S(1)} %get-tuple-element.65), channel_id=1, source_target_pairs={{0,8},{4,12},{8,0},{12,4},{16,24},{20,28},{24,16},{28,20},{1,9},{5... | collective-permute-start | bytes 786440 | tf_op jit(solution)/shard_map/ppermute | solution.py:115
  682.7 41.8 %collective-permute-start.11 = (bf16[256,512]{1,0:T(8,128)(2,1)S(1)}, bf16[256,512]{1,0:T(8,128)(2,1)S(1)}, u32[]{:S(2)}, u32[]{:S(2)}) collective-permute-start(bf16[256,512]{1,0:T(8,128)(2,1)S(1)} %get-tuple-element.63), channel_id=1, source_target_pairs={{0,24},{4,28},{8,16},{12,20},{16,8},{20,12},{24,0},{28,4},{1,25},{... | collective-permute-start | bytes 786440 | tf_op jit(solution)/shard_map/ppermute | solution.py:115
  683.8 44.5 %collective-permute-start.10 = (bf16[256,512]{1,0:T(8,128)(2,1)S(1)}, bf16[256,512]{1,0:T(8,128)(2,1)S(1)}, u32[]{:S(2)}, u32[]{:S(2)}) collective-permute-start(bf16[256,512]{1,0:T(8,128)(2,1)S(1)} %get-tuple-element.64), channel_id=1, source_target_pairs={{0,16},{4,20},{8,24},{12,28},{16,0},{20,4},{24,8},{28,12},{1,17},{... | collective-permute-start | bytes 786440 | tf_op jit(solution)/shard_map/ppermute | solution.py:115
  702.0 26.4 %collective-permute-start.9 = (bf16[256,512]{1,0:T(8,128)(2,1)S(1)}, bf16[256,512]{1,0:T(8,128)(2,1)S(1)}, u32[]{:S(2)}, u32[]{:S(2)}) collective-permute-start(bf16[256,512]{1,0:T(8,128)(2,1)S(1)} %get-tuple-element.62), channel_id=1, source_target_pairs={{0,8},{4,12},{8,0},{12,4},{16,24},{20,28},{24,16},{28,20},{1,9},{5... | collective-permute-start | bytes 786440 | tf_op jit(solution)/shard_map/ppermute | solution.py:115
  705.8 30.0 %collective-permute-start.15 = (bf16[512,256]{1,0:T(8,128)(2,1)S(1)}, bf16[512,256]{1,0:T(8,128)(2,1)S(1)}, u32[]{:S(2)}, u32[]{:S(2)}) collective-permute-start(bf16[512,256]{1,0:T(8,128)(2,1)S(1)} %get-tuple-element.60), channel_id=1, source_target_pairs={{0,24},{4,28},{8,16},{12,20},{16,8},{20,12},{24,0},{28,4},{1,25},{... | collective-permute-start | bytes 786440 | tf_op jit(solution)/shard_map/ppermute | solution.py:115
  706.9 32.7 %collective-permute-start.14 = (bf16[512,256]{1,0:T(8,128)(2,1)S(1)}, bf16[512,256]{1,0:T(8,128)(2,1)S(1)}, u32[]{:S(2)}, u32[]{:S(2)}) collective-permute-start(bf16[512,256]{1,0:T(8,128)(2,1)S(1)} %get-tuple-element.61), channel_id=1, source_target_pairs={{0,16},{4,20},{8,24},{12,28},{16,0},{20,4},{24,8},{28,12},{1,17},{... | collective-permute-start | bytes 786440 | tf_op jit(solution)/shard_map/ppermute | solution.py:115
  724.5 15.1 %collective-permute-start.13 = (bf16[512,256]{1,0:T(8,128)(2,1)S(1)}, bf16[512,256]{1,0:T(8,128)(2,1)S(1)}, u32[]{:S(2)}, u32[]{:S(2)}) collective-permute-start(bf16[512,256]{1,0:T(8,128)(2,1)S(1)} %get-tuple-element.59), channel_id=1, source_target_pairs={{0,8},{4,12},{8,0},{12,4},{16,24},{20,28},{24,16},{28,20},{1,9},{5... | collective-permute-start | bytes 786440 | tf_op jit(solution)/shard_map/ppermute | solution.py:115
  759.2 37.0 %collective-permute-start.16 = (bf16[4,256,512]{2,1,0:T(8,128)(2,1)}, bf16[4,256,512]{2,1,0:T(8,128)(2,1)}, u32[]{:S(2)}, u32[]{:S(2)}) collective-permute-start(bf16[4,256,512]{2,1,0:T(8,128)(2,1)} %fusion.58), channel_id=1, source_target_pairs={{0,4},{4,0},{8,12},{12,8},{16,20},{20,16},{24,28},{28,24},{1,5},{5... | collective-permute-start | bytes 3145736 | tf_op jit(solution)/shard_map/ppermute | solution.py:115
  771.7 32.5 %collective-permute-start.20 = (bf16[4,256,512]{2,1,0:T(8,128)(2,1)}, bf16[4,256,512]{2,1,0:T(8,128)(2,1)S(1)}, u32[]{:S(2)}, u32[]{:S(2)}) collective-permute-start(bf16[4,256,512]{2,1,0:T(8,128)(2,1)} %fusion.59), channel_id=1, source_target_pairs={{0,4},{4,0},{8,12},{12,8},{16,20},{20,16},{24,28},{28,24},{1,5},{5... | collective-permute-start | bytes 3145736 | tf_op jit(solution)/shard_map/ppermute | solution.py:115
  793.8 32.9 %collective-permute-start.24 = (bf16[4,512,256]{2,1,0:T(8,128)(2,1)S(1)}, bf16[4,512,256]{2,1,0:T(8,128)(2,1)S(1)}, u32[]{:S(2)}, u32[]{:S(2)}) collective-permute-start(bf16[4,512,256]{2,1,0:T(8,128)(2,1)S(1)} %bitcast.299), channel_id=1, source_target_pairs={{0,4},{4,0},{8,12},{12,8},{16,20},{20,16},{24,28},{28,24},{1,5},{5... | collective-permute-start | bytes 3145736 | tf_op jit(solution)/shard_map/ppermute | solution.py:115
  798.2 32.3 %collective-permute-start.17 = (bf16[256,512]{1,0:T(8,128)(2,1)S(1)}, bf16[256,512]{1,0:T(8,128)(2,1)S(1)}, u32[]{:S(2)}, u32[]{:S(2)}) collective-permute-start(bf16[256,512]{1,0:T(8,128)(2,1)S(1)} %get-tuple-element.57), channel_id=1, source_target_pairs={{0,8},{4,12},{8,0},{12,4},{16,24},{20,28},{24,16},{28,20},{1,9},{5... | collective-permute-start | bytes 786440 | tf_op jit(solution)/shard_map/ppermute | solution.py:115
  801.3 30.4 %collective-permute-start.18 = (bf16[256,512]{1,0:T(8,128)(2,1)S(1)}, bf16[256,512]{1,0:T(8,128)(2,1)S(1)}, u32[]{:S(2)}, u32[]{:S(2)}) collective-permute-start(bf16[256,512]{1,0:T(8,128)(2,1)S(1)} %get-tuple-element.56), channel_id=1, source_target_pairs={{0,16},{4,20},{8,24},{12,28},{16,0},{20,4},{24,8},{28,12},{1,17},{... | collective-permute-start | bytes 786440 | tf_op jit(solution)/shard_map/ppermute | solution.py:115
  801.4 30.4 %collective-permute-start.19 = (bf16[256,512]{1,0:T(8,128)(2,1)S(1)}, bf16[256,512]{1,0:T(8,128)(2,1)S(1)}, u32[]{:S(2)}, u32[]{:S(2)}) collective-permute-start(bf16[256,512]{1,0:T(8,128)(2,1)S(1)} %get-tuple-element.55), channel_id=1, source_target_pairs={{0,24},{4,28},{8,16},{12,20},{16,8},{20,12},{24,0},{28,4},{1,25},{... | collective-permute-start | bytes 786440 | tf_op jit(solution)/shard_map/ppermute | solution.py:115
  804.8 28.6 %collective-permute-start.21 = (bf16[256,512]{1,0:T(8,128)(2,1)S(1)}, bf16[256,512]{1,0:T(8,128)(2,1)S(1)}, u32[]{:S(2)}, u32[]{:S(2)}) collective-permute-start(bf16[256,512]{1,0:T(8,128)(2,1)S(1)} %get-tuple-element.49), channel_id=1, source_target_pairs={{0,8},{4,12},{8,0},{12,4},{16,24},{20,28},{24,16},{28,20},{1,9},{5... | collective-permute-start | bytes 786440 | tf_op jit(solution)/shard_map/ppermute | solution.py:115
  826.7 22.8 %collective-permute-start.22 = (bf16[256,512]{1,0:T(8,128)(2,1)S(1)}, bf16[256,512]{1,0:T(8,128)(2,1)S(1)}, u32[]{:S(2)}, u32[]{:S(2)}) collective-permute-start(bf16[256,512]{1,0:T(8,128)(2,1)S(1)} %get-tuple-element.48), channel_id=1, source_target_pairs={{0,16},{4,20},{8,24},{12,28},{16,0},{20,4},{24,8},{28,12},{1,17},{... | collective-permute-start | bytes 786440 | tf_op jit(solution)/shard_map/ppermute | solution.py:115
  830.5 34.2 %collective-permute-start.23 = (bf16[256,512]{1,0:T(8,128)(2,1)S(1)}, bf16[256,512]{1,0:T(8,128)(2,1)S(1)}, u32[]{:S(2)}, u32[]{:S(2)}) collective-permute-start(bf16[256,512]{1,0:T(8,128)(2,1)S(1)} %get-tuple-element.47), channel_id=1, source_target_pairs={{0,24},{4,28},{8,16},{12,20},{16,8},{20,12},{24,0},{28,4},{1,25},{... | collective-permute-start | bytes 786440 | tf_op jit(solution)/shard_map/ppermute | solution.py:115
  831.7 33.0 %collective-permute-start.25 = (bf16[512,256]{1,0:T(8,128)(2,1)S(1)}, bf16[512,256]{1,0:T(8,128)(2,1)S(1)}, u32[]{:S(2)}, u32[]{:S(2)}) collective-permute-start(bf16[512,256]{1,0:T(8,128)(2,1)S(1)} %get-tuple-element.41), channel_id=1, source_target_pairs={{0,8},{4,12},{8,0},{12,4},{16,24},{20,28},{24,16},{28,20},{1,9},{5... | collective-permute-start | bytes 786440 | tf_op jit(solution)/shard_map/ppermute | solution.py:115
  831.9 37.3 %collective-permute-start.26 = (bf16[512,256]{1,0:T(8,128)(2,1)S(1)}, bf16[512,256]{1,0:T(8,128)(2,1)S(1)}, u32[]{:S(2)}, u32[]{:S(2)}) collective-permute-start(bf16[512,256]{1,0:T(8,128)(2,1)S(1)} %get-tuple-element.40), channel_id=1, source_target_pairs={{0,16},{4,20},{8,24},{12,28},{16,0},{20,4},{24,8},{28,12},{1,17},{... | collective-permute-start | bytes 786440 | tf_op jit(solution)/shard_map/ppermute | solution.py:115
  833.4 42.5 %collective-permute-start.27 = (bf16[512,256]{1,0:T(8,128)(2,1)S(1)}, bf16[512,256]{1,0:T(8,128)(2,1)S(1)}, u32[]{:S(2)}, u32[]{:S(2)}) collective-permute-start(bf16[512,256]{1,0:T(8,128)(2,1)S(1)} %get-tuple-element.39), channel_id=1, source_target_pairs={{0,24},{4,28},{8,16},{12,20},{16,8},{20,12},{24,0},{28,4},{1,25},{... | collective-permute-start | bytes 786440 | tf_op jit(solution)/shard_map/ppermute | solution.py:115
  (53 other events, 297.3 us)
Sparse Core Ops, SparseCore 0:
  9.6 24.1 all-gather.8
  70.3 32.6 reduce-scatter.4
  106.5 23.0 all-gather.10
  158.2 31.0 reduce-scatter.6
  194.4 22.9 all-gather.12
  250.6 31.0 reduce-scatter.8
  283.9 44.0 all-gather.16
  330.2 23.5 all-gather.14
  356.0 43.6 all-gather.20
  401.2 59.2 all-gather.18
  463.8 30.9 reduce-scatter.10
  496.2 58.7 all-gather.22
where the time goes:
time: 898 us; the launch traced here: 888 us
  waiting for transfers between devices  420 us (47%)
  matrix products  149 us (17%)
  local copies, waits for them, and re-layouts  124 us (14%)
  blocking collectives  82.2 us (9%)
  other arithmetic  56.8 us (6%)
  starting transfers between devices  38.8 us (4%)
  between operations  15.9 us (2%)
    ppermute x28, waiting for transfers between devices, swap(): return lax.ppermute(value, 'dp', [(d, d ^ shift) for d in range(size)])  125 us
    psum x1, blocking collectives, body(): gain_total = lax.psum(gain_stack, ('dp', 'tensor'))  71.2 us
    all_gather x2, waiting for transfers between devices, gather_group(): return lax.all_gather(part, 'tensor', axis=0, tiled=True)  60.7 us
    dot_general x8, matrix products, times_t(): lax.dot_general(left_mat, right_mat, (((1,), (1,)), ((), ())), preferred_...  49.7 us
    all_gather x2, waiting for transfers between devices, gather_group(): lax.all_gather(shard, 'dp', axis=0, tiled=True, axis_index_groups=groups)  45.1 us
    another operation x12, local copies, waits for them, and re-layouts  42.2 us
    ppermute x28, starting transfers between devices, swap(): return lax.ppermute(value, 'dp', [(d, d ^ shift) for d in range(size)])  37.8 us
    dot_general x7, matrix products, t_times(): lax.dot_general(left_mat, right_mat, (((0,), (0,)), ((), ())), preferred_...  36.6 us
  transfers between devices with their start and end apart: 40, of which 24 were waited for; matrix products, arithmetic and copies ran while one was open for 23% of the time, Pallas kernels for 0%

commit v1 on v0

--- a/solution.py
+++ b/solution.py
@@ -183,7 +183,12 @@
     model_width = w_query.shape[0]
     local_width = w_query.shape[1]
     head_count = local_width // HD
-    gathered = lax.all_gather(tokens, "tensor", axis=0, tiled=True)
+    gathered = jnp.concatenate(
+        lax.all_to_all(
+            jnp.stack(lax.axis_size("tensor") * [tokens]), "tensor", split_axis=0, concat_axis=0
+        ),
+        axis=0,
+    )
     row_count = gathered.shape[0]
     segment, offsets = jax.vmap(row_layout)(lengths)
     queries = jnp.dot(gathered, w_query, preferred_element_type=jnp.float32)

time: 898 us -> 902 us (level)
  starting transfers between devices: 38.8 us -> 55.7 us
  waiting for transfers between devices: 420 us -> 408 us
    all_to_all x0 -> x1, waiting for transfers between devices: none -> 22 us  [body(): lax.all_to_all(jnp.stack(lax.axis_size('tensor') * [tokens]), 'tensor', s...]
    all_gather x1 -> x0, waiting for transfers between devices: 21.6 us -> none  [body(): gathered = lax.all_gather(tokens, 'tensor', axis=0, tiled=True)]
    all_gather x1, waiting for transfers between devices: 22.8 us -> 10.7 us  [body(): hidden_all = lax.all_gather(hidden_low, 'tensor', axis=0, tiled=True)]
    reduce_scatter x1, starting transfers between devices: 0.39 us -> 12.4 us  [body(): lax.psum_scatter(jnp.dot(inner_low, w_down, preferred_element_type=jnp.fl...]
    unnamed x130 -> x128, local copies, waits for them, and re-layouts: 34.7 us -> 29.9 us
    another operation x12 -> x13, local copies, waits for them, and re-layouts: 42.2 us -> 42.4 us
where the time goes in v1:
time: 902 us; the launch traced here: 891 us
  waiting for transfers between devices  408 us (45%)
  matrix products  155 us (17%)
  local copies, waits for them, and re-layouts  120 us (13%)
  blocking collectives  82.6 us (9%)
  starting transfers between devices  55.7 us (6%)
  other arithmetic  55.5 us (6%)
  between operations  15.3 us (2%)
    ppermute x28, waiting for transfers between devices, swap(): return lax.ppermute(value, 'dp', [(d, d ^ shift) for d in range(size)])  125 us
    psum x1, blocking collectives, body(): gain_total = lax.psum(gain_stack, ('dp', 'tensor'))  70.8 us
    all_gather x2, waiting for transfers between devices, gather_group(): return lax.all_gather(part, 'tensor', axis=0, tiled=True)  60.9 us
    dot_general x8, matrix products, times_t(): lax.dot_general(left_mat, right_mat, (((1,), (1,)), ((), ())), preferred_...  49.7 us
    all_gather x2, waiting for transfers between devices, gather_group(): lax.all_gather(shard, 'dp', axis=0, tiled=True, axis_index_groups=groups)  44.8 us
    dot_general x7, matrix products, t_times(): lax.dot_general(left_mat, right_mat, (((0,), (0,)), ((), ())), preferred_...  41.3 us
    another operation x12, local copies, waits for them, and re-layouts  39.6 us
    ppermute x28, starting transfers between devices, swap(): return lax.ppermute(value, 'dp', [(d, d ^ shift) for d in range(size)])  37.6 us
  transfers between devices with their start and end apart: 40, of which 24 were waited for; matrix products, arithmetic and copies ran while one was open for 23% of the time, Pallas kernels for 0%

profile of v1, /device:TPU:9, one launch (start us, length us, event | category | flops | bytes accessed | tf_op | source)
XLA Modules:
  0.0 891.1 jit_solution(6461365099941111488)
XLA Ops:
  10.0 5.1 all-to-all-start
  18.0 22.0 %all-to-all-done = bf16[4,128,2048]{2,1,0:T(8,128)(2,1)} async-done(((bf16[4,128,2048]{2,1,0:T(8,128)(2,1)}), bf16[4,128,2048]{2,1,0:T(8,128)(2,1)}, u32[]{:S(2)}, u32[]{:S(2)}) %all-to-all-start) | async-done | bytes 2097184 | tf_op jit(solution)/shard_map/all_to_all | solution.py:187
  51.3 5.9 all-reduce.1
  80.0 32.5 %reduce-scatter.5.cloned.1.call-done = bf16[128,2048]{1,0:T(8,128)(2,1)} async-done(((bf16[512,2048]{1,0:T(8,128)(2,1)}), bf16[128,2048]{1,0:T(8,128)(2,1)}) %reduce-scatter.5.cloned.1.call-update) | async-done | bytes 524304 | tf_op jit(solution)/shard_map/reduce_scatter | solution.py:215
  115.8 12.4 %reduce-scatter.7.cloned.1.call-start = ((), (), s32[]{:S(2)}) async-start(), calls=%async_computation.7 | async-start | bytes 2621440 | tf_op jit(solution)/shard_map/reduce_scatter | solution.py:239
  128.2 10.7 %all-gather.8.cloned.1.call-done = bf16[512,2048]{1,0:T(8,128)(2,1)} async-done(((bf16[128,2048]{1,0:T(8,128)(2,1)}), bf16[512,2048]{1,0:T(8,128)(2,1)}) %all-gather.8.cloned.1.call-update) | async-done | bytes 2097168 | tf_op jit(solution)/shard_map/all_gather | solution.py:225
  138.9 8.6 fusion.92
  147.5 8.4 fusion.93
  158.0 5.8 convolution_convert_fusion
  163.9 31.1 %reduce-scatter.7.cloned.1.call-done = bf16[128,2048]{1,0:T(8,128)(2,1)} async-done(((bf16[512,2048]{1,0:T(8,128)(2,1)}), bf16[128,2048]{1,0:T(8,128)(2,1)}) %reduce-scatter.7.cloned.1.call-update) | async-done | bytes 524304 | tf_op jit(solution)/shard_map/reduce_scatter | solution.py:239
  200.1 23.1 %all-gather.10.cloned.1.call-done = bf16[512,2048]{1,0:T(8,128)(2,1)} async-done(((bf16[128,2048]{1,0:T(8,128)(2,1)}), bf16[512,2048]{1,0:T(8,128)(2,1)}) %all-gather.10.cloned.1.call-update) | async-done | bytes 2097168 | tf_op jit(solution)/shard_map/all_gather | solution.py:251
  223.2 7.6 fusion.94
  230.8 13.6 %fusion.25 = f32[512,2048]{1,0:T(8,128)} fusion(bf16[2048,2048]{1,0:T(8,128)(2,1)} %param.20, f32[512,2048]{1,0:T(8,128)} %copy-done.50, f32[512,2048]{1,0:T(8,128)S(1)} %fusion.94, f32[512,2048]{1,0:T(8,128)} %copy-done.51), kind=kOutput, calls=%fused_computation.56 | convolution fusion | flops 4305453056 | bytes 25165824 | tf_op jit(solution)/shard_map/dot_general | solution.py:48
  244.5 11.8 %add_convert_fusion.1 = bf16[512,2048]{1,0:T(8,128)(2,1)} fusion(f32[512,2048]{1,0:T(8,128)} %fusion.25, bf16[2048,2048]{1,0:T(8,128)(2,1)} %param.21, f32[512,2048]{1,0:T(8,128)S(1)} %fusion.94, f32[512,2048]{1,0:T(8,128)} %copy-done.50), kind=kOutput, calls=%fused_computation.8 | convolution fusion | flops 4303355904 | bytes 23068672 | tf_op jit(solution)/shard_map/dot_general | solution.py:48
  256.9 30.6 %reduce-scatter.9.cloned.1.call-done = bf16[128,2048]{1,0:T(8,128)(2,1)} async-done(((bf16[512,2048]{1,0:T(8,128)(2,1)}), bf16[128,2048]{1,0:T(8,128)(2,1)}) %reduce-scatter.9.cloned.1.call-update) | async-done | bytes 524304 | tf_op jit(solution)/shard_map/reduce_scatter | solution.py:278
  292.7 40.9 %all-gather.14.cloned.1.call-done = bf16[512,2048]{1,0:T(8,128)(2,1)} async-done(((bf16[128,2048]{1,0:T(8,128)(2,1)}), bf16[512,2048]{1,0:T(8,128)(2,1)}) %all-gather.14.cloned.1.call-update) | async-done | bytes 2097168 | tf_op jit(solution)/shard_map/all_gather | solution.py:231
  334.0 25.5 %all-gather.12.cloned.1.call-done = bf16[512,2048]{1,0:T(8,128)(2,1)} async-done(((bf16[128,2048]{1,0:T(8,128)(2,1)}), bf16[512,2048]{1,0:T(8,128)(2,1)}) %all-gather.12.cloned.1.call-update) | async-done | bytes 2097168 | tf_op jit(solution)/shard_map/all_gather | solution.py:285
  383.6 5.9 all-reduce
  405.5 60.9 %all-gather.16.cloned.1.call-done = bf16[2048,2048]{1,0:T(8,128)(2,1)} async-done(((bf16[512,2048]{1,0:T(8,128)(2,1)}), bf16[2048,2048]{1,0:T(8,128)(2,1)}) %all-gather.16.cloned.1.call-update) | async-done | bytes 8388624 | tf_op jit(solution)/shard_map/all_gather | solution.py:232
  466.4 10.6 %fusion.14 = f32[2048,512]{1,0:T(8,128)} fusion(bf16[2048,2048]{1,0:T(8,128)(2,1)} %all-gather.16.cloned.1.call-done, bf16[2048,2048]{1,0:T(8,128)(2,1)} %param.20, s32[]{:T(128)S(6)} %select_n.141), kind=kOutput, calls=%fused_computation.44 | convolution fusion | flops 4294967296 | bytes 14680068 | tf_op jit(solution)/shard_map/dot_general | solution.py:262
  477.0 8.1 fusion.18
  485.1 4.8 convolution_bitcast_fusion.2
  489.9 6.6 reshape.578
  506.1 4.9 convolution_bitcast_fusion.1
  511.0 6.9 reshape.579
  526.5 4.8 convolution_bitcast_fusion
  531.3 6.8 reshape.580
  559.1 70.8 %psum.39 = f32[4,2048]{1,0:T(4,128)S(1)} all-reduce(f32[4,2048]{1,0:T(4,128)S(1)} %pad_maximum_fusion.8), channel_id=1, replica_groups=mesh['dp'=8,'tensor'=4] {'dp','tensor'}, use_global_device_ids=true, to_apply=%region_26.27 | all-reduce | flops 8192 | bytes 65536 | tf_op jit(solution)/shard_map/psum | solution.py:328
  630.5 5.4 constant_dynamic-slice_fusion.5
  636.6 4.4 copy.71
  641.0 6.0 copy.73
  647.0 4.6 copy.75
  666.5 5.4 collective-permute-done.3
  671.9 14.5 %collective-permute-done.2 = bf16[256,512]{1,0:T(8,128)(2,1)S(1)} collective-permute-done((bf16[256,512]{1,0:T(8,128)(2,1)S(1)}, bf16[256,512]{1,0:T(8,128)(2,1)S(1)}, u32[]{:S(2)}, u32[]{:S(2)}) %collective-permute-start.2) | collective-permute-done | bytes 262176 | tf_op jit(solution)/shard_map/ppermute | solution.py:115
  687.6 4.6 collective-permute-start.10
  692.1 13.7 %collective-permute-done.7 = bf16[256,512]{1,0:T(8,128)(2,1)S(1)} collective-permute-done((bf16[256,512]{1,0:T(8,128)(2,1)S(1)}, bf16[256,512]{1,0:T(8,128)(2,1)S(1)}, u32[]{:S(2)}, u32[]{:S(2)}) %collective-permute-start.7) | collective-permute-done | bytes 262176 | tf_op jit(solution)/shard_map/ppermute | solution.py:115
  714.8 13.6 %collective-permute-done.11 = bf16[256,512]{1,0:T(8,128)(2,1)S(1)} collective-permute-done((bf16[256,512]{1,0:T(8,128)(2,1)S(1)}, bf16[256,512]{1,0:T(8,128)(2,1)S(1)}, u32[]{:S(2)}, u32[]{:S(2)}) %collective-permute-start.11) | collective-permute-done | bytes 262176 | tf_op jit(solution)/shard_map/ppermute | solution.py:115
  733.1 6.5 collective-permute-done.15
  746.5 7.8 fusion.20
  754.3 7.6 fusion.26
  764.0 8.3 fusion.4
  776.3 9.7 %fusion.5 = f32[512,2048]{1,0:T(8,128)} fusion(bf16[2048,2048]{1,0:T(8,128)(2,1)S(1)} %bitcast.320, f32[2048,512]{1,0:T(8,128)} %fusion.18, f32[2048,512]{1,0:T(8,128)} %fusion.14), kind=kOutput, calls=%fused_computation.25 | convolution fusion | flops 4301258752 | bytes 20971520 | tf_op jit(solution)/shard_map/dot_general | solution.py:54
  786.0 6.8 reshape.583
  811.6 18.9 %collective-permute-done.24 = bf16[4,512,256]{2,1,0:T(8,128)(2,1)S(1)} collective-permute-done((bf16[4,512,256]{2,1,0:T(8,128)(2,1)S(1)}, bf16[4,512,256]{2,1,0:T(8,128)(2,1)S(1)}, u32[]{:S(2)}, u32[]{:S(2)}) %collective-permute-start.24) | collective-permute-done | bytes 1048608 | tf_op jit(solution)/shard_map/ppermute | solution.py:115
  838.3 14.9 %collective-permute-done.22 = bf16[256,512]{1,0:T(8,128)(2,1)S(1)} collective-permute-done((bf16[256,512]{1,0:T(8,128)(2,1)S(1)}, bf16[256,512]{1,0:T(8,128)(2,1)S(1)}, u32[]{:S(2)}, u32[]{:S(2)}) %collective-permute-start.22) | collective-permute-done | bytes 262176 | tf_op jit(solution)/shard_map/ppermute | solution.py:115
  853.3 15.1 %collective-permute-done.23 = bf16[256,512]{1,0:T(8,128)(2,1)S(1)} collective-permute-done((bf16[256,512]{1,0:T(8,128)(2,1)S(1)}, bf16[256,512]{1,0:T(8,128)(2,1)S(1)}, u32[]{:S(2)}, u32[]{:S(2)}) %collective-permute-start.23) | collective-permute-done | bytes 262176 | tf_op jit(solution)/shard_map/ppermute | solution.py:115
  868.5 4.4 collective-permute-done.26
  873.0 6.6 collective-permute-done.27
  (309 shorter events, 210.4 us)
Async XLA Ops:
  7.2 37.1 %copy-start = (bf16[2048,512]{1,0:T(8,128)(2,1)S(1)}, bf16[2048,512]{1,0:T(8,128)(2,1)}, u32[]{:S(2)}) copy-start(bf16[2048,512]{1,0:T(8,128)(2,1)} %param.16) | copy-start | bytes 6291460
  10.0 30.0 %all-to-all-start = ((bf16[4,128,2048]{2,1,0:T(8,128)(2,1)}), bf16[4,128,2048]{2,1,0:T(8,128)(2,1)}, u32[]{:S(2)}, u32[]{:S(2)}) async-start(bf16[4,128,2048]{2,1,0:T(8,128)(2,1)} %stack.22), calls=%async_computation | async-start | bytes 4194304 | tf_op jit(solution)/shard_map/all_to_all | solution.py:187
  15.0 97.4 %reduce-scatter.5.cloned.1.call-start = ((), (), s32[]{:S(2)}) async-start(), calls=%async_computation.5 | async-start | bytes 2621440 | tf_op jit(solution)/shard_map/reduce_scatter | solution.py:215
  76.3 37.3 %copy-start.40 = (bf16[4,128,512]{2,1,0:T(8,128)(2,1)}, bf16[4,128,512]{2,1,0:T(8,128)(2,1)S(1)}, u32[]{:S(2)}) copy-start(bf16[4,128,512]{2,1,0:T(8,128)(2,1)S(1)} %fusion.40) | copy-start | bytes 1572868
  77.3 36.4 %copy-start.16 = (bf16[128,2048]{1,0:T(8,128)(2,1)S(1)}, bf16[128,2048]{1,0:T(8,128)(2,1)}, u32[]{:S(2)}) copy-start(bf16[128,2048]{1,0:T(8,128)(2,1)} %param.14) | copy-start | bytes 1572868
  77.3 36.4 %copy-start.42 = (f32[2048]{0:T(1024)S(1)}, f32[2048]{0:T(1024)}, u32[]{:S(2)}) copy-start(f32[2048]{0:T(1024)} %param.25) | copy-start | bytes 24580
  79.9 59.0 %all-gather.8.cloned.1.call-start = ((), (), s32[]{:S(2)}) async-start(), calls=%async_computation.6 | async-start | bytes 2621440 | tf_op jit(solution)/shard_map/all_gather | solution.py:225
  115.8 79.3 %reduce-scatter.7.cloned.1.call-start = ((), (), s32[]{:S(2)}) async-start(), calls=%async_computation.7 | async-start | bytes 2621440 | tf_op jit(solution)/shard_map/reduce_scatter | solution.py:239
  158.0 38.3 %copy-start.8 = (bf16[128,2048]{1,0:T(8,128)(2,1)S(1)}, bf16[128,2048]{1,0:T(8,128)(2,1)}, u32[]{:S(2)}) copy-start(bf16[128,2048]{1,0:T(8,128)(2,1)} %param.27) | copy-start | bytes 1572868
  158.0 38.3 %copy-start.43 = (f32[2048]{0:T(1024)S(1)}, f32[2048]{0:T(1024)}, u32[]{:S(2)}) copy-start(f32[2048]{0:T(1024)} %param.26) | copy-start | bytes 24580
  163.9 59.3 %all-gather.10.cloned.1.call-start = ((), (), s32[]{:S(2)}) async-start(), calls=%async_computation.8 | async-start | bytes 2621440 | tf_op jit(solution)/shard_map/all_gather | solution.py:251
  200.1 87.4 %reduce-scatter.9.cloned.1.call-start = ((), (), s32[]{:S(2)}) async-start(), calls=%async_computation.9 | async-start | bytes 2621440 | tf_op jit(solution)/shard_map/reduce_scatter | solution.py:278
  244.5 43.0 %copy-start.13 = (bf16[128,2048]{1,0:T(8,128)(2,1)S(1)}, bf16[128,2048]{1,0:T(8,128)(2,1)}, u32[]{:S(2)}) copy-start(bf16[128,2048]{1,0:T(8,128)(2,1)} %reduce-scatter.5.cloned.1.call-done) | copy-start | bytes 1572868
  256.3 77.4 %all-gather.14.cloned.1.call-start = ((), (), s32[]{:S(2)}) async-start(), calls=%async_computation.12 | async-start | bytes 2621440 | tf_op jit(solution)/shard_map/all_gather | solution.py:231
  256.9 102.6 %all-gather.12.cloned.1.call-start = ((), (), s32[]{:S(2)}) async-start(), calls=%async_computation.10 | async-start | bytes 2621440 | tf_op jit(solution)/shard_map/all_gather | solution.py:285
  291.9 113.5 %all-gather.18.cloned.1.call-start = ((), (), s32[]{:S(2)}) async-start(), calls=%async_computation.14 | async-start | bytes 2621440 | tf_op jit(solution)/shard_map/all_gather | solution.py:231
  292.7 173.7 %all-gather.16.cloned.1.call-start = ((), (), s32[]{:S(2)}) async-start(), calls=%async_computation.13 | async-start | bytes 10485760 | tf_op jit(solution)/shard_map/all_gather | solution.py:232
  333.7 410.7 %reduce-scatter.11.cloned.1.call-start = ((), (), s32[]{:S(2)}) async-start(), calls=%async_computation.11 | async-start | bytes 2621440 | tf_op jit(solution)/shard_map/reduce_scatter | solution.py:312
  401.5 345.0 %all-gather.20.cloned.1.call-start = ((), (), s32[]{:S(2)}) async-start(), calls=%async_computation.15 | async-start | bytes 10485760 | tf_op jit(solution)/shard_map/all_gather | solution.py:232
  504.9 147.3 %collective-permute-start = (bf16[4,256,512]{2,1,0:T(8,128)(2,1)}, bf16[4,256,512]{2,1,0:T(8,128)(2,1)}, u32[]{:S(2)}, u32[]{:S(2)}) collective-permute-start(bf16[4,256,512]{2,1,0:T(8,128)(2,1)} %bitcast.299), channel_id=1, source_target_pairs={{0,4},{4,0},{8,12},{12,8},{16,20},{20,16},{24,28},{28,24},{1,5},{5... | collective-permute-start | bytes 3145736 | tf_op jit(solution)/shard_map/ppermute | solution.py:115
  526.2 131.7 %collective-permute-start.4 = (bf16[4,256,512]{2,1,0:T(8,128)(2,1)}, bf16[4,256,512]{2,1,0:T(8,128)(2,1)}, u32[]{:S(2)}, u32[]{:S(2)}) collective-permute-start(bf16[4,256,512]{2,1,0:T(8,128)(2,1)} %bitcast.298), channel_id=1, source_target_pairs={{0,4},{4,0},{8,12},{12,8},{16,20},{20,16},{24,28},{28,24},{1,5},{5... | collective-permute-start | bytes 3145736 | tf_op jit(solution)/shard_map/ppermute | solution.py:115
  546.3 113.4 %collective-permute-start.8 = (bf16[4,256,512]{2,1,0:T(8,128)(2,1)}, bf16[4,256,512]{2,1,0:T(8,128)(2,1)}, u32[]{:S(2)}, u32[]{:S(2)}) collective-permute-start(bf16[4,256,512]{2,1,0:T(8,128)(2,1)} %bitcast.297), channel_id=1, source_target_pairs={{0,4},{4,0},{8,12},{12,8},{16,20},{20,16},{24,28},{28,24},{1,5},{5... | collective-permute-start | bytes 3145736 | tf_op jit(solution)/shard_map/ppermute | solution.py:115
  552.8 108.9 %collective-permute-start.12 = (bf16[4,512,256]{2,1,0:T(8,128)(2,1)}, bf16[4,512,256]{2,1,0:T(8,128)(2,1)}, u32[]{:S(2)}, u32[]{:S(2)}) collective-permute-start(bf16[4,512,256]{2,1,0:T(8,128)(2,1)} %fusion.56), channel_id=1, source_target_pairs={{0,4},{4,0},{8,12},{12,8},{16,20},{20,16},{24,28},{28,24},{1,5},{5... | collective-permute-start | bytes 3145736 | tf_op jit(solution)/shard_map/ppermute | solution.py:115
  654.5 17.4 %collective-permute-start.3 = (bf16[256,512]{1,0:T(8,128)(2,1)S(1)}, bf16[256,512]{1,0:T(8,128)(2,1)S(1)}, u32[]{:S(2)}, u32[]{:S(2)}) collective-permute-start(bf16[256,512]{1,0:T(8,128)(2,1)S(1)} %get-tuple-element.69), channel_id=1, source_target_pairs={{0,24},{4,28},{8,16},{12,20},{16,8},{20,12},{24,0},{28,4},{1,25},{... | collective-permute-start | bytes 786440 | tf_op jit(solution)/shard_map/ppermute | solution.py:115
  654.9 31.6 %collective-permute-start.2 = (bf16[256,512]{1,0:T(8,128)(2,1)S(1)}, bf16[256,512]{1,0:T(8,128)(2,1)S(1)}, u32[]{:S(2)}, u32[]{:S(2)}) collective-permute-start(bf16[256,512]{1,0:T(8,128)(2,1)S(1)} %get-tuple-element.70), channel_id=1, source_target_pairs={{0,16},{4,20},{8,24},{12,28},{16,0},{20,4},{24,8},{28,12},{1,17},{... | collective-permute-start | bytes 786440 | tf_op jit(solution)/shard_map/ppermute | solution.py:115
  657.9 29.7 %collective-permute-start.1 = (bf16[256,512]{1,0:T(8,128)(2,1)S(1)}, bf16[256,512]{1,0:T(8,128)(2,1)S(1)}, u32[]{:S(2)}, u32[]{:S(2)}) collective-permute-start(bf16[256,512]{1,0:T(8,128)(2,1)S(1)} %get-tuple-element.68), channel_id=1, source_target_pairs={{0,8},{4,12},{8,0},{12,4},{16,24},{20,28},{24,16},{28,20},{1,9},{5... | collective-permute-start | bytes 786440 | tf_op jit(solution)/shard_map/ppermute | solution.py:115
  659.7 46.1 %collective-permute-start.7 = (bf16[256,512]{1,0:T(8,128)(2,1)S(1)}, bf16[256,512]{1,0:T(8,128)(2,1)S(1)}, u32[]{:S(2)}, u32[]{:S(2)}) collective-permute-start(bf16[256,512]{1,0:T(8,128)(2,1)S(1)} %get-tuple-element.66), channel_id=1, source_target_pairs={{0,24},{4,28},{8,16},{12,20},{16,8},{20,12},{24,0},{28,4},{1,25},{... | collective-permute-start | bytes 786440 | tf_op jit(solution)/shard_map/ppermute | solution.py:115
  661.7 48.0 %collective-permute-start.6 = (bf16[256,512]{1,0:T(8,128)(2,1)S(1)}, bf16[256,512]{1,0:T(8,128)(2,1)S(1)}, u32[]{:S(2)}, u32[]{:S(2)}) collective-permute-start(bf16[256,512]{1,0:T(8,128)(2,1)S(1)} %get-tuple-element.67), channel_id=1, source_target_pairs={{0,16},{4,20},{8,24},{12,28},{16,0},{20,4},{24,8},{28,12},{1,17},{... | collective-permute-start | bytes 786440 | tf_op jit(solution)/shard_map/ppermute | solution.py:115
  666.5 77.9 %copy-start.19 = (bf16[128,2048]{1,0:T(8,128)(2,1)S(1)}, bf16[128,2048]{1,0:T(8,128)(2,1)}, u32[]{:S(2)}) copy-start(bf16[128,2048]{1,0:T(8,128)(2,1)} %reduce-scatter.9.cloned.1.call-done) | copy-start | bytes 1572868
  671.9 38.9 %collective-permute-start.5 = (bf16[256,512]{1,0:T(8,128)(2,1)S(1)}, bf16[256,512]{1,0:T(8,128)(2,1)S(1)}, u32[]{:S(2)}, u32[]{:S(2)}) collective-permute-start(bf16[256,512]{1,0:T(8,128)(2,1)S(1)} %get-tuple-element.65), channel_id=1, source_target_pairs={{0,8},{4,12},{8,0},{12,4},{16,24},{20,28},{24,16},{28,20},{1,9},{5... | collective-permute-start | bytes 786440 | tf_op jit(solution)/shard_map/ppermute | solution.py:115
  686.5 41.9 %collective-permute-start.11 = (bf16[256,512]{1,0:T(8,128)(2,1)S(1)}, bf16[256,512]{1,0:T(8,128)(2,1)S(1)}, u32[]{:S(2)}, u32[]{:S(2)}) collective-permute-start(bf16[256,512]{1,0:T(8,128)(2,1)S(1)} %get-tuple-element.63), channel_id=1, source_target_pairs={{0,24},{4,28},{8,16},{12,20},{16,8},{20,12},{24,0},{28,4},{1,25},{... | collective-permute-start | bytes 786440 | tf_op jit(solution)/shard_map/ppermute | solution.py:115
  687.6 44.6 %collective-permute-start.10 = (bf16[256,512]{1,0:T(8,128)(2,1)S(1)}, bf16[256,512]{1,0:T(8,128)(2,1)S(1)}, u32[]{:S(2)}, u32[]{:S(2)}) collective-permute-start(bf16[256,512]{1,0:T(8,128)(2,1)S(1)} %get-tuple-element.64), channel_id=1, source_target_pairs={{0,16},{4,20},{8,24},{12,28},{16,0},{20,4},{24,8},{28,12},{1,17},{... | collective-permute-start | bytes 786440 | tf_op jit(solution)/shard_map/ppermute | solution.py:115
  705.8 26.4 %collective-permute-start.9 = (bf16[256,512]{1,0:T(8,128)(2,1)S(1)}, bf16[256,512]{1,0:T(8,128)(2,1)S(1)}, u32[]{:S(2)}, u32[]{:S(2)}) collective-permute-start(bf16[256,512]{1,0:T(8,128)(2,1)S(1)} %get-tuple-element.62), channel_id=1, source_target_pairs={{0,8},{4,12},{8,0},{12,4},{16,24},{20,28},{24,16},{28,20},{1,9},{5... | collective-permute-start | bytes 786440 | tf_op jit(solution)/shard_map/ppermute | solution.py:115
  709.7 30.0 %collective-permute-start.15 = (bf16[512,256]{1,0:T(8,128)(2,1)S(1)}, bf16[512,256]{1,0:T(8,128)(2,1)S(1)}, u32[]{:S(2)}, u32[]{:S(2)}) collective-permute-start(bf16[512,256]{1,0:T(8,128)(2,1)S(1)} %get-tuple-element.60), channel_id=1, source_target_pairs={{0,24},{4,28},{8,16},{12,20},{16,8},{20,12},{24,0},{28,4},{1,25},{... | collective-permute-start | bytes 786440 | tf_op jit(solution)/shard_map/ppermute | solution.py:115
  710.8 32.7 %collective-permute-start.14 = (bf16[512,256]{1,0:T(8,128)(2,1)S(1)}, bf16[512,256]{1,0:T(8,128)(2,1)S(1)}, u32[]{:S(2)}, u32[]{:S(2)}) collective-permute-start(bf16[512,256]{1,0:T(8,128)(2,1)S(1)} %get-tuple-element.61), channel_id=1, source_target_pairs={{0,16},{4,20},{8,24},{12,28},{16,0},{20,4},{24,8},{28,12},{1,17},{... | collective-permute-start | bytes 786440 | tf_op jit(solution)/shard_map/ppermute | solution.py:115
  728.4 15.1 %collective-permute-start.13 = (bf16[512,256]{1,0:T(8,128)(2,1)S(1)}, bf16[512,256]{1,0:T(8,128)(2,1)S(1)}, u32[]{:S(2)}, u32[]{:S(2)}) collective-permute-start(bf16[512,256]{1,0:T(8,128)(2,1)S(1)} %get-tuple-element.59), channel_id=1, source_target_pairs={{0,8},{4,12},{8,0},{12,4},{16,24},{20,28},{24,16},{28,20},{1,9},{5... | collective-permute-start | bytes 786440 | tf_op jit(solution)/shard_map/ppermute | solution.py:115
  763.0 36.9 %collective-permute-start.16 = (bf16[4,256,512]{2,1,0:T(8,128)(2,1)}, bf16[4,256,512]{2,1,0:T(8,128)(2,1)}, u32[]{:S(2)}, u32[]{:S(2)}) collective-permute-start(bf16[4,256,512]{2,1,0:T(8,128)(2,1)} %fusion.58), channel_id=1, source_target_pairs={{0,4},{4,0},{8,12},{12,8},{16,20},{20,16},{24,28},{28,24},{1,5},{5... | collective-permute-start | bytes 3145736 | tf_op jit(solution)/shard_map/ppermute | solution.py:115
  775.4 32.6 %collective-permute-start.20 = (bf16[4,256,512]{2,1,0:T(8,128)(2,1)}, bf16[4,256,512]{2,1,0:T(8,128)(2,1)S(1)}, u32[]{:S(2)}, u32[]{:S(2)}) collective-permute-start(bf16[4,256,512]{2,1,0:T(8,128)(2,1)} %fusion.59), channel_id=1, source_target_pairs={{0,4},{4,0},{8,12},{12,8},{16,20},{20,16},{24,28},{28,24},{1,5},{5... | collective-permute-start | bytes 3145736 | tf_op jit(solution)/shard_map/ppermute | solution.py:115
  797.4 33.1 %collective-permute-start.24 = (bf16[4,512,256]{2,1,0:T(8,128)(2,1)S(1)}, bf16[4,512,256]{2,1,0:T(8,128)(2,1)S(1)}, u32[]{:S(2)}, u32[]{:S(2)}) collective-permute-start(bf16[4,512,256]{2,1,0:T(8,128)(2,1)S(1)} %bitcast.300), channel_id=1, source_target_pairs={{0,4},{4,0},{8,12},{12,8},{16,20},{20,16},{24,28},{28,24},{1,5},{5... | collective-permute-start | bytes 3145736 | tf_op jit(solution)/shard_map/ppermute | solution.py:115
  801.8 32.4 %collective-permute-start.17 = (bf16[256,512]{1,0:T(8,128)(2,1)S(1)}, bf16[256,512]{1,0:T(8,128)(2,1)S(1)}, u32[]{:S(2)}, u32[]{:S(2)}) collective-permute-start(bf16[256,512]{1,0:T(8,128)(2,1)S(1)} %get-tuple-element.57), channel_id=1, source_target_pairs={{0,8},{4,12},{8,0},{12,4},{16,24},{20,28},{24,16},{28,20},{1,9},{5... | collective-permute-start | bytes 786440 | tf_op jit(solution)/shard_map/ppermute | solution.py:115
  804.9 30.5 %collective-permute-start.18 = (bf16[256,512]{1,0:T(8,128)(2,1)S(1)}, bf16[256,512]{1,0:T(8,128)(2,1)S(1)}, u32[]{:S(2)}, u32[]{:S(2)}) collective-permute-start(bf16[256,512]{1,0:T(8,128)(2,1)S(1)} %get-tuple-element.56), channel_id=1, source_target_pairs={{0,16},{4,20},{8,24},{12,28},{16,0},{20,4},{24,8},{28,12},{1,17},{... | collective-permute-start | bytes 786440 | tf_op jit(solution)/shard_map/ppermute | solution.py:115
  805.1 30.5 %collective-permute-start.19 = (bf16[256,512]{1,0:T(8,128)(2,1)S(1)}, bf16[256,512]{1,0:T(8,128)(2,1)S(1)}, u32[]{:S(2)}, u32[]{:S(2)}) collective-permute-start(bf16[256,512]{1,0:T(8,128)(2,1)S(1)} %get-tuple-element.55), channel_id=1, source_target_pairs={{0,24},{4,28},{8,16},{12,20},{16,8},{20,12},{24,0},{28,4},{1,25},{... | collective-permute-start | bytes 786440 | tf_op jit(solution)/shard_map/ppermute | solution.py:115
  808.5 28.6 %collective-permute-start.21 = (bf16[256,512]{1,0:T(8,128)(2,1)S(1)}, bf16[256,512]{1,0:T(8,128)(2,1)S(1)}, u32[]{:S(2)}, u32[]{:S(2)}) collective-permute-start(bf16[256,512]{1,0:T(8,128)(2,1)S(1)} %get-tuple-element.49), channel_id=1, source_target_pairs={{0,8},{4,12},{8,0},{12,4},{16,24},{20,28},{24,16},{28,20},{1,9},{5... | collective-permute-start | bytes 786440 | tf_op jit(solution)/shard_map/ppermute | solution.py:115
  830.5 22.8 %collective-permute-start.22 = (bf16[256,512]{1,0:T(8,128)(2,1)S(1)}, bf16[256,512]{1,0:T(8,128)(2,1)S(1)}, u32[]{:S(2)}, u32[]{:S(2)}) collective-permute-start(bf16[256,512]{1,0:T(8,128)(2,1)S(1)} %get-tuple-element.48), channel_id=1, source_target_pairs={{0,16},{4,20},{8,24},{12,28},{16,0},{20,4},{24,8},{28,12},{1,17},{... | collective-permute-start | bytes 786440 | tf_op jit(solution)/shard_map/ppermute | solution.py:115
  834.2 34.2 %collective-permute-start.23 = (bf16[256,512]{1,0:T(8,128)(2,1)S(1)}, bf16[256,512]{1,0:T(8,128)(2,1)S(1)}, u32[]{:S(2)}, u32[]{:S(2)}) collective-permute-start(bf16[256,512]{1,0:T(8,128)(2,1)S(1)} %get-tuple-element.47), channel_id=1, source_target_pairs={{0,24},{4,28},{8,16},{12,20},{16,8},{20,12},{24,0},{28,4},{1,25},{... | collective-permute-start | bytes 786440 | tf_op jit(solution)/shard_map/ppermute | solution.py:115
  835.4 33.0 %collective-permute-start.25 = (bf16[512,256]{1,0:T(8,128)(2,1)S(1)}, bf16[512,256]{1,0:T(8,128)(2,1)S(1)}, u32[]{:S(2)}, u32[]{:S(2)}) collective-permute-start(bf16[512,256]{1,0:T(8,128)(2,1)S(1)} %get-tuple-element.41), channel_id=1, source_target_pairs={{0,8},{4,12},{8,0},{12,4},{16,24},{20,28},{24,16},{28,20},{1,9},{5... | collective-permute-start | bytes 786440 | tf_op jit(solution)/shard_map/ppermute | solution.py:115
  835.6 37.3 %collective-permute-start.26 = (bf16[512,256]{1,0:T(8,128)(2,1)S(1)}, bf16[512,256]{1,0:T(8,128)(2,1)S(1)}, u32[]{:S(2)}, u32[]{:S(2)}) collective-permute-start(bf16[512,256]{1,0:T(8,128)(2,1)S(1)} %get-tuple-element.40), channel_id=1, source_target_pairs={{0,16},{4,20},{8,24},{12,28},{16,0},{20,4},{24,8},{28,12},{1,17},{... | collective-permute-start | bytes 786440 | tf_op jit(solution)/shard_map/ppermute | solution.py:115
  837.2 42.5 %collective-permute-start.27 = (bf16[512,256]{1,0:T(8,128)(2,1)S(1)}, bf16[512,256]{1,0:T(8,128)(2,1)S(1)}, u32[]{:S(2)}, u32[]{:S(2)}) collective-permute-start(bf16[512,256]{1,0:T(8,128)(2,1)S(1)} %get-tuple-element.39), channel_id=1, source_target_pairs={{0,24},{4,28},{8,16},{12,20},{16,8},{20,12},{24,0},{28,4},{1,25},{... | collective-permute-start | bytes 786440 | tf_op jit(solution)/shard_map/ppermute | solution.py:115
  (52 other events, 314.2 us)
Sparse Core Ops, SparseCore 0:
  80.0 32.3 reduce-scatter.4
  115.9 22.9 all-gather.7
  164.0 31.0 reduce-scatter.6
  200.2 22.9 all-gather.9
  256.4 31.0 reduce-scatter.8
  289.5 44.0 all-gather.13
  335.9 23.5 all-gather.11
  361.7 43.6 all-gather.17
  407.0 59.2 all-gather.15
  469.5 30.9 reduce-scatter.10
  502.1 58.7 all-gather.19
